TPU v7x, 32 devices: a whole 2x2x4 slice. The times are simulated.
32 devices in a mesh: bag: 4 (over y, x), seq: 8 (over z, core).
Axes of the slice: x: 2, y: 2, z: 4, core: 2. Of those that a mesh axis runs over, the one named last changes fastest.
Arguments:
- text_rows: bfloat16 [2048, 3072], P(('bag', 'seq')), may hold values from -6 to 6
- image_rows: bfloat16 [1024, 3072], P(('bag', 'seq')), may hold values from -6 to 6
- modulation: float32 [32, 2, 2, 3072], P('bag'), may hold values from -3 to 3
- head_weight: bfloat16 [2, 3072, 6144], P(None, None, 'seq'), may hold values from -0.109375 to 0.109375
- norm_gain: float32 [2, 2, 128], replicated, may hold values from 0.5 to 20
- store_down: bfloat16 [128, 2, 64, 3072], P('bag', None, 'seq'), may hold values from -0.109375 to 0.109375
- store_up: bfloat16 [128, 2, 64, 6144], P('bag', None, None, 'seq'), may hold values from -0.375 to 0.375
- store_row: int32 [128], replicated, may hold values from 0 to 127, as said below
- user_adapter: int32 [4, 4], replicated, may hold values from 0 to 127, as said below
- image_lengths: int32 [4, 4], P('bag'), may hold values from 1 to 64, 128 in all within a row
Outputs:
- text_out: bfloat16 [2048, 2048], P(('bag', 'seq'))
- image_out: bfloat16 [1024, 2048], P(('bag', 'seq'))
Inputs may be any that keep to these rules, and one draw needn't show every extreme that they name: A permutation: adapter a is kept at row store_row[a] of store_down and store_up, whose owner is store_row[a] // 32. `user_adapter`: the 4 users of one bag have adapters kept by 4 different owners, so every owner keeps exactly one adapter of each bag.
All inputs are finite; a program needn't handle non-finite values.
Results may differ from a plain program's by a relative error of at most 0.04.
The roundings to bfloat16 on the way count: a program that leaves them out, or rounds other values in their place, can miss the bound.
Values may be sent and summed in bfloat16 or wider, within the bound.
No kernel may reach another device: no remote copies, remote signals or barrier semaphores. Data moves between devices by JAX's collectives and lax.ppermute only.
A program may use at most 128 MiB of HBM per device.

v0:
```python
import math
import jax
import jax.numpy as jnp
from jax import lax
from jax.sharding import PartitionSpec as P

HEAD_DIM = 128
TEXT = 64


def modulate(raw_rows, shifts, scales):
    values = raw_rows.astype(jnp.float32)
    centre = values - jnp.mean(values, axis=-1, keepdims=True)
    spread = jnp.mean(centre * centre, axis=-1, keepdims=True)
    normed = centre * lax.rsqrt(spread + 1e-06)
    return ((1.0 + scales) * normed + shifts).astype(jnp.bfloat16)


def head_normed(values, gain_row):
    spread = jnp.mean(values * values, axis=-1, keepdims=True)
    return (values * lax.rsqrt(spread + 1e-06) * gain_row).astype(jnp.bfloat16)


def attend(queries, keys_all, values_all, seg_ids):
    row_total = queries.shape[0]
    block_rows = math.gcd(row_total, 1024)
    query_blocks = queries.reshape(row_total // block_rows, block_rows, queries.shape[1])
    seg_blocks = seg_ids.reshape(row_total // block_rows, block_rows)
    factor = 1.0 / math.sqrt(queries.shape[1])

    def one_block(block_pair):
        query_rows, query_segs = block_pair
        scores = jnp.dot(query_rows, keys_all.T, preferred_element_type=jnp.float32) * factor
        scores = jnp.where(query_segs[:, None] == seg_ids[None, :], scores, -1e30)
        top_score = jnp.max(scores, axis=1, keepdims=True)
        weights = jnp.exp(scores - top_score)
        prob_rows = (weights / jnp.sum(weights, axis=1, keepdims=True)).astype(jnp.bfloat16)
        return jnp.dot(prob_rows, values_all, preferred_element_type=jnp.float32).astype(
            jnp.bfloat16
        )

    return lax.map(one_block, (query_blocks, seg_blocks)).reshape(row_total, values_all.shape[1])


def user_table(user_ids, user_count):
    return user_ids[:, None] == jnp.arange(user_count, dtype=jnp.int32)[None, :]


def pick_rows(seg_pick, table_rows):
    return jnp.dot(seg_pick, table_rows, precision=lax.Precision.HIGHEST)


def part_ranks(hidden_all, down_part, user_ids, user_count):
    all_users = jnp.einsum("nd,urd->urn", hidden_all, down_part, preferred_element_type=jnp.float32)
    user_pick = user_table(user_ids, user_count).astype(jnp.float32).T
    return jnp.sum(all_users * user_pick[:, None, :], axis=0).astype(jnp.bfloat16)


def adapted(hidden_all, weight, ranks, up_users, user_ids, gain_pair):
    row_count = hidden_all.shape[0]
    user_count = up_users.shape[0]
    plain_part = jnp.dot(hidden_all, weight, preferred_element_type=jnp.float32)
    user_pick = user_table(user_ids, user_count).astype(jnp.bfloat16)
    spread_ranks = (user_pick[:, :, None] * ranks[:, None, :]).reshape(row_count, -1)
    adjust = jnp.dot(
        spread_ranks, up_users.reshape(-1, weight.shape[1]), preferred_element_type=jnp.float32
    )
    heads_here = weight.shape[1] // (3 * HEAD_DIM)
    mixed_cols = (plain_part + adjust).reshape(row_count, heads_here, 3, HEAD_DIM)
    query = head_normed(mixed_cols[:, :, 0], gain_pair[0])
    key_rows = head_normed(mixed_cols[:, :, 1], gain_pair[1])
    value_rows = mixed_cols[:, :, 2].astype(jnp.bfloat16)
    return (query, key_rows, value_rows)


def body(
    text_rows,
    image_rows,
    modulation,
    head_weight,
    norm_gain,
    store_down,
    store_up,
    store_row,
    user_adapter,
    image_lengths,
):
    seq_count = lax.axis_size("seq")
    bag_index = lax.axis_index("bag")
    seq_index = lax.axis_index("seq")
    text_dev = text_rows.shape[0]
    image_dev = image_rows.shape[0]
    text_bag = text_dev * seq_count
    image_bag = image_dev * seq_count
    user_count = image_lengths.shape[1]
    seg_count = modulation.shape[0]
    store_size = store_down.shape[0]
    seg_ends = jnp.cumsum(jnp.repeat(image_lengths[0], 2))
    text_segs = jnp.arange(text_bag, dtype=jnp.int32) // TEXT
    image_segs = jnp.sum(
        (jnp.arange(image_bag, dtype=jnp.int32)[:, None] >= seg_ends[None, :]).astype(jnp.int32),
        axis=1,
    )
    seg_range = jnp.arange(seg_count, dtype=jnp.int32)
    text_local = lax.dynamic_slice_in_dim(text_segs, seq_index * text_dev, text_dev)
    image_local = lax.dynamic_slice_in_dim(image_segs, seq_index * image_dev, image_dev)
    text_pick = (text_local[:, None] == seg_range[None, :]).astype(jnp.float32)
    image_pick = (image_local[:, None] == seg_range[None, :]).astype(jnp.float32)
    text_hidden = modulate(
        text_rows,
        pick_rows(text_pick, modulation[:, 0, 0]),
        pick_rows(text_pick, modulation[:, 0, 1]),
    )
    image_hidden = modulate(
        image_rows,
        pick_rows(image_pick, modulation[:, 1, 0]),
        pick_rows(image_pick, modulation[:, 1, 1]),
    )
    store_rows = jnp.take(store_row, user_adapter, axis=0)
    owners = store_rows // store_size
    owner_match = owners == bag_index
    sending = jnp.any(owner_match, axis=1)
    slot_index = jnp.sum(jnp.where(owner_match, store_rows % store_size, 0), axis=1)
    down_send = jnp.where(
        sending[:, None, None, None],
        jnp.take(store_down, slot_index, axis=0),
        jnp.zeros((), jnp.bfloat16),
    )
    up_send = jnp.where(
        sending[:, None, None, None],
        jnp.take(store_up, slot_index, axis=0),
        jnp.zeros((), jnp.bfloat16),
    )
    down_recv, up_recv = (
        lax.all_to_all(down_send, "bag", split_axis=0, concat_axis=0, tiled=True),
        lax.all_to_all(up_send, "bag", split_axis=0, concat_axis=0, tiled=True),
    )
    my_owners = lax.dynamic_index_in_dim(owners, bag_index, 0, keepdims=False)
    down_users = jnp.take(down_recv, my_owners, axis=0)
    up_users = jnp.take(up_recv, my_owners, axis=0)
    text_all, image_all = (
        lax.all_gather(text_hidden, "seq", axis=0, tiled=True),
        lax.all_gather(image_hidden, "seq", axis=0, tiled=True),
    )
    text_part = part_ranks(text_all, down_users[:, 0], text_segs // 2, user_count)
    image_part = part_ranks(image_all, down_users[:, 1], image_segs // 2, user_count)
    text_cols, image_cols = (
        lax.all_gather(text_part, "seq", axis=0, tiled=True),
        lax.all_gather(image_part, "seq", axis=0, tiled=True),
    )
    text_rank_all = text_cols.T
    image_rank_all = image_cols.T
    text_parts = adapted(
        text_all, head_weight[0], text_rank_all, up_users[:, 0], text_segs // 2, norm_gain[0]
    )
    image_parts = adapted(
        image_all, head_weight[1], image_rank_all, up_users[:, 1], image_segs // 2, norm_gain[1]
    )
    joined = [
        jnp.transpose(jnp.concatenate([text_parts[which], image_parts[which]], axis=0), (1, 0, 2))
        for which in range(3)
    ]
    seg_all = jnp.concatenate([text_segs, image_segs], axis=0)

    def one_head(head_rows):
        return attend(head_rows[0], head_rows[1], head_rows[2], seg_all)

    outputs = lax.map(one_head, (joined[0], joined[1], joined[2]))
    heads_here = outputs.shape[0]
    outputs = jnp.transpose(outputs, (1, 0, 2)).reshape(text_bag + image_bag, heads_here * HEAD_DIM)
    text_out, image_out = (
        lax.all_to_all(outputs[:text_bag], "seq", split_axis=0, concat_axis=1, tiled=True),
        lax.all_to_all(outputs[text_bag:], "seq", split_axis=0, concat_axis=1, tiled=True),
    )
    return (text_out, image_out)


def solution(mesh):
    in_specs = (
        P(("bag", "seq"), None),
        P(("bag", "seq"), None),
        P("bag", None, None, None),
        P(None, None, "seq"),
        P(),
        P("bag", None, "seq", None),
        P("bag", None, None, "seq"),
        P(),
        P(),
        P("bag", None),
    )
    out_specs = (P(("bag", "seq"), None), P(("bag", "seq"), None))
    return jax.shard_map(body, mesh=mesh, in_specs=in_specs, out_specs=out_specs, check_vma=False)
```

profile of v0, /device:TPU:0, one launch (start us, length us, event | category | flops | bytes accessed | tf_op | source)
XLA Modules:
  0.0 189.1 jit_solution(12241190175673804232)
XLA Ops:
  10.7 2.2 %fusion.64 = (f32[8,1,1,3072]{3,2,1,0:T(1,128)}, f32[8,1,1,3072]{3,2,1,0:T(1,128)S(1)}, f32[8,1,1,3072]{3,2,1,0:T(1,128)}, f32[8,1,1,3072]{3,2,1,0:T(1,128)}) fusion(f32[8,2,2,3072]{3,2,1,0:T(2,128)} %param.16), kind=kLoop, calls=%fused_computation.163 | loop fusion | bytes 786432 | tf_op jit(solution)/shard_map/slice | solution.py:111
  14.4 2.0 %fusion.16 = bf16[32,3072]{1,0:T(8,128)(2,1)} fusion(f32[32,3072]{1,0:T(8,128)S(1)} %fusion.15, f32[8,1,1,3072]{3,2,1,0:T(1,128)} %get-tuple-element.146, s32[32]{0:T(128)S(1)} %dynamic_slice.30), kind=kOutput, calls=%fused_computation.34 | convolution fusion | flops 9634048 | bytes 688256 | tf_op jit(solution)/shard_map/dot_general | solution.py:50
  24.4 5.2 %all-to-all-start = ((bf16[4,2,8,3072]{3,2,1,0:T(8,128)(2,1)}), bf16[4,2,8,3072]{3,2,1,0:T(8,128)(2,1)}, u32[]{:S(2)}, u32[]{:S(2)}) async-start(bf16[4,2,8,3072]{3,2,1,0:T(8,128)(2,1)} %copy.93), calls=%async_computation | async-start | bytes 786432 | tf_op jit(solution)/shard_map/all_to_all | solution.py:135
  30.1 1.5 fusion.13
  31.6 2.2 %fusion.14 = bf16[64,3072]{1,0:T(8,128)(2,1)} fusion(f32[64,3072]{1,0:T(8,128)S(1)} %fusion.13, f32[8,1,1,3072]{3,2,1,0:T(1,128)} %get-tuple-element.143, s32[64]{0:T(128)S(1)} %dynamic_slice.28), kind=kOutput, calls=%fused_computation.30 | convolution fusion | flops 19268096 | bytes 1278208 | tf_op jit(solution)/shard_map/dot_general | solution.py:50
  38.4 4.5 %gather_fusion.3 = bf16[4,2,64,768]{3,2,1,0:T(8,128)(2,1)} fusion(bf16[32,2,64,768]{3,2,1,0:T(8,128)(2,1)} %param.20, s32[1024]{0:T(1024)} %copy-done.13), kind=kCustom, calls=%fused_computation.3 | custom fusion | bytes 1572880 | tf_op jit(solution)/shard_map/jit(_take)/gather | solution.py:131
  42.9 2.2 %select_select_fusion = bf16[4,2,64,768]{3,2,1,0:T(8,128)(2,1)} fusion(bf16[4,2,64,768]{3,2,1,0:T(8,128)(2,1)} %gather_fusion.3, pred[4]{0:T(512)(128)(4,1)S(1)} %copy-done.19, pred[4]{0:T(512)(128)(4,1)} %copy-done.15), kind=kLoop, calls=%fused_computation.50 | loop fusion | flops 786432 | bytes 1572872 | tf_op jit(solution)/shard_map/jit(_where)/select_n | solution.py:129
  45.1 4.2 %all-to-all-start.1 = ((bf16[4,2,64,768]{3,2,1,0:T(8,128)(2,1)}), bf16[4,2,64,768]{3,2,1,0:T(8,128)(2,1)}, u32[]{:S(2)}, u32[]{:S(2)}) async-start(bf16[4,2,64,768]{3,2,1,0:T(8,128)(2,1)} %select_select_fusion), calls=%async_computation.1 | async-start | bytes 1572864 | tf_op jit(solution)/shard_map/all_to_all | solution.py:136
  49.3 2.3 %gather_fusion.2 = bf16[4,2,8,3072]{3,2,1,0:T(8,128)(2,1)} fusion(bf16[4,2,8,3072]{3,2,1,0:T(8,128)(2,1)} %all-to-all-done, s32[1024]{0:T(1024)S(1)} %pad_clamp_fusion), kind=kCustom, calls=%fused_computation.2 | custom fusion | bytes 786448 | tf_op jit(solution)/shard_map/jit(_take)/gather | solution.py:139
  52.7 8.0 %all-to-all-done.1 = bf16[4,2,64,768]{3,2,1,0:T(8,128)(2,1)} async-done(((bf16[4,2,64,768]{3,2,1,0:T(8,128)(2,1)}), bf16[4,2,64,768]{3,2,1,0:T(8,128)(2,1)}, u32[]{:S(2)}, u32[]{:S(2)}) %all-to-all-start.1) | async-done | bytes 786464 | tf_op jit(solution)/shard_map/all_to_all | solution.py:136
  60.7 2.8 %gather_fusion.4 = bf16[4,2,64,768]{3,2,1,0:T(8,128)(2,1)} fusion(bf16[4,2,64,768]{3,2,1,0:T(8,128)(2,1)} %all-to-all-done.1, s32[1024]{0:T(1024)} %copy-done.14), kind=kCustom, calls=%fused_computation.4 | custom fusion | bytes 1572880 | tf_op jit(solution)/shard_map/jit(_take)/gather | solution.py:140
  65.7 2.0 %fusion.30 = bf16[8,256]{1,0:T(8,128)(2,1)S(1)} fusion(bf16[256,3072]{1,0:T(8,128)(2,1)} %all-gather.5.cloned.1.call-done, bf16[4,2,8,3072]{3,2,0,1:T(8,128)(2,1)S(1)} %copy_select_fusion, f32[4,256]{1,0:T(4,128)S(1)} %fusion.49), kind=kOutput, calls=%fused_computation.44 | convolution fusion | flops 50345984 | bytes 1777664 | tf_op jit(solution)/shard_map/nd,urd->urn/dot_general | solution.py:54
  67.7 14.8 %all_gather.15 = bf16[64,256]{1,0:T(8,128)(2,1)S(1)} all-gather(bf16[8,256]{1,0:T(8,128)(2,1)S(1)} %fusion.30), channel_id=1, replica_groups=mesh['bag'=4,'seq'=8] {'seq'}, dimensions={0}, use_global_device_ids=true | all-gather | bytes 36864 | tf_op jit(solution)/shard_map/all_gather | solution.py:149
  83.2 4.2 %fusion.7 = f32[256,768]{1,0:T(8,128)S(1)} fusion(bf16[256,3072]{1,0:T(8,128)(2,1)} %all-gather.5.cloned.1.call-done, bf16[2,3072,768]{2,1,0:T(8,128)(2,1)} %param.17), kind=kOutput, calls=%fused_computation.21 | convolution fusion | flops 1207959552 | bytes 7077888 | tf_op jit(solution)/shard_map/dot_general | solution.py:62
  88.6 2.3 %copy.98 = f32[256,768]{0,1:T(8,128)} copy(f32[256,768]{1,0:T(8,128)} %convolution_add_fusion.5) | data formatting | bytes 1572864 | tf_op jit(solution)/shard_map/add | solution.py:69
  92.1 1.6 fusion.41
  93.7 1.5 multiply_convert_fusion.2
  95.2 3.1 %fusion.24 = bf16[8,512]{1,0:T(8,128)(2,1)S(1)} fusion(bf16[512,3072]{1,0:T(8,128)(2,1)} %all-gather.3.cloned.1.call-done, bf16[4,2,8,3072]{3,2,0,1:T(8,128)(2,1)S(1)} %copy_select_fusion, f32[4,512]{1,0:T(4,128)S(1)} %fusion.47), kind=kOutput, calls=%fused_computation.42 | convolution fusion | flops 100691968 | bytes 3358720 | tf_op jit(solution)/shard_map/nd,urd->urn/dot_general | solution.py:54
  98.3 14.2 %all_gather.13 = bf16[64,512]{1,0:T(8,128)(2,1)S(1)} all-gather(bf16[8,512]{1,0:T(8,128)(2,1)S(1)} %fusion.24), channel_id=1, replica_groups=mesh['bag'=4,'seq'=8] {'seq'}, dimensions={0}, use_global_device_ids=true | all-gather | bytes 73728 | tf_op jit(solution)/shard_map/all_gather | solution.py:148
  112.5 5.0 %fusion.9 = f32[512,768]{1,0:T(8,128)S(1)} fusion(bf16[512,3072]{1,0:T(8,128)(2,1)S(1)} %copy-done.3, bf16[2,3072,768]{2,1,0:T(8,128)(2,1)} %param.17), kind=kOutput, calls=%fused_computation.23 | convolution fusion | flops 2415919104 | bytes 9437184 | tf_op jit(solution)/shard_map/dot_general | solution.py:62
  117.6 1.6 convolution_add_fusion.4
  119.1 3.1 %copy.95 = f32[512,768]{0,1:T(8,128)} copy(f32[512,768]{1,0:T(8,128)} %convolution_add_fusion.4) | data formatting | bytes 3145728 | tf_op jit(solution)/shard_map/add | solution.py:69
  122.2 1.4 multiply_reduce_fusion
  128.4 26.8 %while.23 = (s32[]{:T(128)}, bf16[2,768,128]{2,1,0:T(8,128)(2,1)}, bf16[2,768,128]{1,2,0:T(8,128)(2,1)}, s32[768]{0:T(1024)S(1)}, bf16[2,768,128]{1,2,0:T(8,128)...) while((s32[]{:T(128)}, bf16[2,768,128]{2,1,0:T(8,128)(2,1)}, ...), condition=%wide.wide.region_19.20_spmd, body=%wide.wide.region_14.19_spmd.sunk | while | flops 102465024 | bytes 5647666 | solution.py:168
  132.2 8.0 %while.24 = (s32[]{:T(128)}, bf16[3,256,128]{2,1,0:T(8,128)(2,1)}, s32[3,256]{1,0:T(4,128)S(1)}, s32[768]{0:T(1024)S(1)}, bf16[3,256,128]{2,1,0:T(8,128)(2,1)}, ...) while((s32[]{:T(128)}, bf16[3,256,128]{2,1,0:T(8,128)(2,1)}, ...), condition=%wide.region_18.18_spmd, body=%wide.region_15.17_spmd.sunk | while | flops 102465024 | bytes 2894953 | solution.py:42
  140.2 1.6 bitcast_dynamic-update-slice_fusion.3
  145.6 8.0 %while.24 = (s32[]{:T(128)}, bf16[3,256,128]{2,1,0:T(8,128)(2,1)}, s32[3,256]{1,0:T(4,128)S(1)}, s32[768]{0:T(1024)S(1)}, bf16[3,256,128]{2,1,0:T(8,128)(2,1)}, ...) while((s32[]{:T(128)}, bf16[3,256,128]{2,1,0:T(8,128)(2,1)}, ...), condition=%wide.region_18.18_spmd, body=%wide.region_15.17_spmd.sunk | while | flops 102465024 | bytes 2894953 | solution.py:42
  153.6 1.6 bitcast_dynamic-update-slice_fusion.3
  157.0 4.7 %all-to-all-start.3 = ((bf16[8,32,256]{2,1,0:T(8,128)(2,1)}), bf16[8,32,256]{2,1,0:T(8,128)(2,1)S(1)}, u32[]{:S(2)}, u32[]{:S(2)}) async-start(bf16[8,32,256]{2,1,0:T(8,128)(2,1)} %all_to_all.40), calls=%async_computation.3 | async-start | bytes 262144 | tf_op jit(solution)/shard_map/all_to_all | solution.py:173
  163.9 4.6 %all-to-all-done.3 = bf16[8,32,256]{2,1,0:T(8,128)(2,1)S(1)} async-done(((bf16[8,32,256]{2,1,0:T(8,128)(2,1)}), bf16[8,32,256]{2,1,0:T(8,128)(2,1)S(1)}, u32[]{:S(2)}, u32[]{:S(2)}) %all-to-all-start.3) | async-done | bytes 131104 | tf_op jit(solution)/shard_map/all_to_all | solution.py:173
  168.5 3.4 %all-to-all-start.2 = ((bf16[8,64,256]{2,1,0:T(8,128)(2,1)}), bf16[8,64,256]{2,1,0:T(8,128)(2,1)S(1)}, u32[]{:S(2)}, u32[]{:S(2)}) async-start(bf16[8,64,256]{2,1,0:T(8,128)(2,1)} %all_to_all.36), calls=%async_computation.2 | async-start | bytes 524288 | tf_op jit(solution)/shard_map/all_to_all | solution.py:172
  172.6 9.0 %all-to-all-done.2 = bf16[8,64,256]{2,1,0:T(8,128)(2,1)S(1)} async-done(((bf16[8,64,256]{2,1,0:T(8,128)(2,1)}), bf16[8,64,256]{2,1,0:T(8,128)(2,1)S(1)}, u32[]{:S(2)}, u32[]{:S(2)}) %all-to-all-start.2) | async-done | bytes 262176 | tf_op jit(solution)/shard_map/all_to_all | solution.py:172
  (156 shorter events, 57.9 us)
Async XLA Ops:
  7.2 13.4 %copy-start = (bf16[32,2,8,3072]{3,2,1,0:T(8,128)(2,1)S(1)}, bf16[32,2,8,3072]{3,2,1,0:T(8,128)(2,1)}, u32[]{:S(2)}) copy-start(bf16[32,2,8,3072]{3,2,1,0:T(8,128)(2,1)} %param.19) | copy-start | bytes 9437188
  7.2 12.0 %copy-start.9 = (s32[4,4]{1,0:T(4,128)S(1)}, s32[4,4]{1,0:T(4,128)}, u32[]{:S(2)}) copy-start(s32[4,4]{1,0:T(4,128)} %param.22) | copy-start | bytes 196
  7.2 11.2 %copy-start.1 = (s32[128]{0:T(128)S(1)}, s32[128]{0:T(128)}, u32[]{:S(2)}) copy-start(s32[128]{0:T(128)} %param.21) | copy-start | bytes 1540
  7.2 58.5 %all-gather.5.cloned.1.call-start = ((), (), s32[]{:S(2)}) async-start(), calls=%async_computation.5 | async-start | bytes 1769472 | tf_op jit(solution)/shard_map/all_gather | solution.py:143
  10.7 2.3 %copy-start.16 = (s32[256]{0:T(256)}, s32[256]{0:T(256)S(1)}, u32[]{:S(2)}) copy-start(s32[256]{0:T(256)S(1)} %convert_reduce_fusion.2) | copy-start | bytes 3076
  14.4 15.3 %copy-start.2 = (bf16[64,3072]{1,0:T(8,128)(2,1)S(1)}, bf16[64,3072]{1,0:T(8,128)(2,1)}, u32[]{:S(2)}) copy-start(bf16[64,3072]{1,0:T(8,128)(2,1)} %param.14) | copy-start | bytes 1179652
  19.9 13.9 %copy-start.15 = (pred[4]{0:T(512)(128)(4,1)}, pred[4]{0:T(512)(128)(4,1)S(1)}, u32[]{:S(2)}) copy-start(pred[4]{0:T(512)(128)(4,1)S(1)} %get-tuple-element.130) | copy-start | bytes 16
  20.0 0.5 copy-start.22
  20.5 13.3 %copy-start.13 = (s32[1024]{0:T(1024)}, s32[1024]{0:T(1024)S(1)}, u32[]{:S(2)}) copy-start(s32[1024]{0:T(1024)S(1)} %pad_clamp_fusion.1) | copy-start | bytes 12292
  21.9 12.0 %copy-start.17 = (s32[256]{0:T(256)S(1)}, s32[256]{0:T(256)}, u32[]{:S(2)}) copy-start(s32[256]{0:T(256)} %copy-done.16) | copy-start | bytes 3076
  22.5 7.1 %copy-start.18 = (pred[4]{0:T(512)(128)(4,1)}, pred[4]{0:T(512)(128)(4,1)S(1)}, u32[]{:S(2)}) copy-start(pred[4]{0:T(512)(128)(4,1)S(1)} %compare_and_fusion) | copy-start | bytes 16
  24.4 20.7 %all-to-all-start = ((bf16[4,2,8,3072]{3,2,1,0:T(8,128)(2,1)}), bf16[4,2,8,3072]{3,2,1,0:T(8,128)(2,1)}, u32[]{:S(2)}, u32[]{:S(2)}) async-start(bf16[4,2,8,3072]{3,2,1,0:T(8,128)(2,1)} %copy.93), calls=%async_computation | async-start | bytes 786432 | tf_op jit(solution)/shard_map/all_to_all | solution.py:135
  29.6 65.6 %all-gather.3.cloned.1.call-start = ((), (), s32[]{:S(2)}) async-start(), calls=%async_computation.4 | async-start | bytes 3538944 | tf_op jit(solution)/shard_map/all_gather | solution.py:142
  31.6 11.3 %copy-start.19 = (pred[4]{0:T(512)(128)(4,1)S(1)}, pred[4]{0:T(512)(128)(4,1)}, u32[]{:S(2)}) copy-start(pred[4]{0:T(512)(128)(4,1)} %copy-done.18) | copy-start | bytes 16
  33.9 15.4 %copy-start.10 = (s32[768]{0:T(1024)}, s32[768]{0:T(1024)S(1)}, u32[]{:S(2)}) copy-start(s32[768]{0:T(1024)S(1)} %pad_add_fusion) | copy-start | bytes 9220
  34.6 14.7 %copy-start.14 = (s32[1024]{0:T(1024)}, s32[1024]{0:T(1024)S(1)}, u32[]{:S(2)}) copy-start(s32[1024]{0:T(1024)S(1)} %pad_clamp_fusion) | copy-start | bytes 12292
  45.1 15.6 %all-to-all-start.1 = ((bf16[4,2,64,768]{3,2,1,0:T(8,128)(2,1)}), bf16[4,2,64,768]{3,2,1,0:T(8,128)(2,1)}, u32[]{:S(2)}, u32[]{:S(2)}) async-start(bf16[4,2,64,768]{3,2,1,0:T(8,128)(2,1)} %select_select_fusion), calls=%async_computation.1 | async-start | bytes 1572864 | tf_op jit(solution)/shard_map/all_to_all | solution.py:136
  83.2 4.3 %copy-start.5 = (bf16[4,1,64,768]{3,2,1,0:T(8,128)(2,1)S(1)}, bf16[4,1,64,768]{3,2,1,0:T(8,128)(2,1)}, u32[]{:S(2)}) copy-start(bf16[4,1,64,768]{3,2,1,0:T(8,128)(2,1)} %get-tuple-element.142) | copy-start | bytes 1179652
  90.9 21.6 %copy-start.12 = (bf16[512,4]{0,1:T(4,128)(2,1)S(1)}, bf16[512,4]{0,1:T(4,128)(2,1)}, u32[]{:S(2)}) copy-start(bf16[512,4]{0,1:T(4,128)(2,1)} %fusion.46) | copy-start | bytes 12292
  95.2 17.3 %copy-start.3 = (bf16[512,3072]{1,0:T(8,128)(2,1)S(1)}, bf16[512,3072]{1,0:T(8,128)(2,1)}, u32[]{:S(2)}) copy-start(bf16[512,3072]{1,0:T(8,128)(2,1)} %all-gather.3.cloned.1.call-done) | copy-start | bytes 9437188
  112.5 5.0 %copy-start.4 = (bf16[4,1,64,768]{3,2,1,0:T(8,128)(2,1)S(1)}, bf16[4,1,64,768]{3,2,1,0:T(8,128)(2,1)}, u32[]{:S(2)}) copy-start(bf16[4,1,64,768]{3,2,1,0:T(8,128)(2,1)} %get-tuple-element.141) | copy-start | bytes 1179652
  119.1 5.6 %copy-start.20 = (f32[128]{0:T(128)S(1)}, f32[128]{0:T(128)}, u32[]{:S(2)}) copy-start(f32[128]{0:T(128)} %get-tuple-element.147) | copy-start | bytes 1540
  119.1 5.6 %copy-start.21 = (f32[128]{0:T(128)S(1)}, f32[128]{0:T(128)}, u32[]{:S(2)}) copy-start(f32[128]{0:T(128)} %get-tuple-element.149) | copy-start | bytes 1540
  119.1 6.9 %copy-start.8 = (bf16[256,2,128]{0,2,1:T(8,128)(2,1)S(1)}, bf16[256,2,128]{0,2,1:T(8,128)(2,1)}, u32[]{:S(2)}) copy-start(bf16[256,2,128]{0,2,1:T(8,128)(2,1)} %get-tuple-element.151) | copy-start | bytes 393220
  119.1 7.7 %copy-start.6 = (bf16[256,2,128]{0,2,1:T(8,128)(2,1)S(1)}, bf16[256,2,128]{0,2,1:T(8,128)(2,1)}, u32[]{:S(2)}) copy-start(bf16[256,2,128]{0,2,1:T(8,128)(2,1)} %fusion.41) | copy-start | bytes 393220
  122.2 5.4 %copy-start.7 = (bf16[256,2,128]{0,2,1:T(8,128)(2,1)S(1)}, bf16[256,2,128]{0,2,1:T(8,128)(2,1)}, u32[]{:S(2)}) copy-start(bf16[256,2,128]{0,2,1:T(8,128)(2,1)} %get-tuple-element.152) | copy-start | bytes 393220
  122.2 6.2 %copy-start.11 = (s32[768]{0:T(1024)S(1)}, s32[768]{0:T(1024)}, u32[]{:S(2)}) copy-start(s32[768]{0:T(1024)} %copy-done.10) | copy-start | bytes 9220
  157.0 11.5 %all-to-all-start.3 = ((bf16[8,32,256]{2,1,0:T(8,128)(2,1)}), bf16[8,32,256]{2,1,0:T(8,128)(2,1)S(1)}, u32[]{:S(2)}, u32[]{:S(2)}) async-start(bf16[8,32,256]{2,1,0:T(8,128)(2,1)} %all_to_all.40), calls=%async_computation.3 | async-start | bytes 262144 | tf_op jit(solution)/shard_map/all_to_all | solution.py:173
  168.5 13.1 %all-to-all-start.2 = ((bf16[8,64,256]{2,1,0:T(8,128)(2,1)}), bf16[8,64,256]{2,1,0:T(8,128)(2,1)S(1)}, u32[]{:S(2)}, u32[]{:S(2)}) async-start(bf16[8,64,256]{2,1,0:T(8,128)(2,1)} %all_to_all.36), calls=%async_computation.2 | async-start | bytes 524288 | tf_op jit(solution)/shard_map/all_to_all | solution.py:172
Sparse Core Ops, SparseCore 0:
  16.5 27.9 all-gather.4
  46.2 37.7 all-gather.2
where the time goes:
time: 191 us; the launch traced here: 189 us
  local copies, waits for them, and re-layouts  44.5 us (23%)
  matrix products  38.2 us (20%)
  blocking collectives  29 us (15%)
  other arithmetic  23.8 us (12%)
  waiting for transfers between devices  21.6 us (11%)
  starting transfers between devices  17.6 us (9%)
  between operations  14.4 us (8%)
    all_gather x1, blocking collectives, body(): lax.all_gather(image_part, 'seq', axis=0, tiled=True)  14.8 us
    all_gather x1, blocking collectives, body(): lax.all_gather(text_part, 'seq', axis=0, tiled=True)  14.2 us
    dot_general x2, matrix products, adapted(): plain_part = jnp.dot(hidden_all, weight, preferred_element_type=jnp.float32)  9.25 us
    all_to_all x1, waiting for transfers between devices, body(): lax.all_to_all(outputs[:text_bag], 'seq', split_axis=0, concat_axis=1, ti...  8.97 us
    all_to_all x1, waiting for transfers between devices, body(): lax.all_to_all(up_send, 'bag', split_axis=0, concat_axis=0, tiled=True)  7.96 us
    dot_general x6, matrix products, one_block(): jnp.dot(query_rows, keys_all.T, preferred_element_type=jnp.float32) * factor  7.93 us
    dynamic_slice x10, local copies, waits for them, and re-layouts, body(): outputs = lax.map(one_head, (joined[0], joined[1], joined[2]))  7.58 us
    dot_general x4, matrix products, pick_rows(): return jnp.dot(seg_pick, table_rows, precision=lax.Precision.HIGHEST)  6.94 us
  transfers between devices with their start and end apart: 6, of which 3 were waited for; matrix products, arithmetic and copies ran while one was open for 25% of the time, Pallas kernels for 0%

commit v1 on v0

--- a/solution.py
+++ b/solution.py
@@ -6,6 +6,13 @@
 
 HEAD_DIM = 128
 TEXT = 64
+
+
+def trade_parts(x, mesh_axis, split, join):
+    size = lax.axis_size(mesh_axis)
+    parts = jnp.stack(jnp.split(x, size, axis=split), axis=0)
+    parts = lax.all_to_all(parts, mesh_axis, split_axis=0, concat_axis=0)
+    return jnp.concatenate(parts, axis=join)
 
 
 def modulate(raw_rows, shifts, scales):
@@ -169,7 +176,7 @@
     heads_here = outputs.shape[0]
     outputs = jnp.transpose(outputs, (1, 0, 2)).reshape(text_bag + image_bag, heads_here * HEAD_DIM)
     text_out, image_out = (
-        lax.all_to_all(outputs[:text_bag], "seq", split_axis=0, concat_axis=1, tiled=True),
+        trade_parts(outputs[:text_bag], "seq", 0, 1),
         lax.all_to_all(outputs[text_bag:], "seq", split_axis=0, concat_axis=1, tiled=True),
     )
     return (text_out, image_out)

time: 191 us -> 206 us (1.079)
  local copies, waits for them, and re-layouts: 44.5 us -> 61.8 us
  waiting for transfers between devices: 21.6 us -> 17 us
    another operation x1 -> x10, local copies, waits for them, and re-layouts: 0.08 us -> 7.45 us  [the longest x9 7.36 us: trade_parts(): parts = jnp.stack(jnp.split(x, size, axis=split), axis=0)]
    split x0 -> x9, local copies, waits for them, and re-layouts: none -> 6.06 us  [trade_parts(): parts = jnp.stack(jnp.split(x, size, axis=split), axis=0)]
    unnamed x46 -> x55, local copies, waits for them, and re-layouts: 0.6 us -> 6.64 us
    all_to_all x1, waiting for transfers between devices: 4.63 us -> 0.01 us  [body(): lax.all_to_all(outputs[text_bag:], 'seq', split_axis=0, concat_axis=1, ti...]
  transfers between devices with their start and end apart: 6 -> 6, of which waited for: 3 -> 2; matrix products, arithmetic and copies ran while one was open for 25% -> 31% of each run, Pallas kernels for 0% -> 0%
where the time goes in v1:
time: 206 us; the launch traced here: 203 us
  local copies, waits for them, and re-layouts  61.8 us (30%)
  matrix products  38.2 us (19%)
  blocking collectives  29.1 us (14%)
  other arithmetic  23.8 us (12%)
  starting transfers between devices  19.2 us (9%)
  waiting for transfers between devices  17 us (8%)
  between operations  14.4 us (7%)
    all_gather x1, blocking collectives, body(): lax.all_gather(image_part, 'seq', axis=0, tiled=True)  14.9 us
    all_gather x1, blocking collectives, body(): lax.all_gather(text_part, 'seq', axis=0, tiled=True)  14.2 us
    dot_general x2, matrix products, adapted(): plain_part = jnp.dot(hidden_all, weight, preferred_element_type=jnp.float32)  9.24 us
    all_to_all x1, waiting for transfers between devices, trade_parts(): parts = lax.all_to_all(parts, mesh_axis, split_axis=0, concat_axis=0)  9.05 us
    all_to_all x1, waiting for transfers between devices, body(): lax.all_to_all(up_send, 'bag', split_axis=0, concat_axis=0, tiled=True)  7.95 us
    dot_general x6, matrix products, one_block(): jnp.dot(query_rows, keys_all.T, preferred_element_type=jnp.float32) * factor  7.93 us
    dynamic_slice x10, local copies, waits for them, and re-layouts, body(): outputs = lax.map(one_head, (joined[0], joined[1], joined[2]))  7.58 us
    another operation x9, local copies, waits for them, and re-layouts, trade_parts(): parts = jnp.stack(jnp.split(x, size, axis=split), axis=0)  7.36 us
  transfers between devices with their start and end apart: 6, of which 2 were waited for; matrix products, arithmetic and copies ran while one was open for 31% of the time, Pallas kernels for 0%

profile of v1, /device:TPU:0, one launch (start us, length us, event | category | flops | bytes accessed | tf_op | source)
XLA Modules:
  0.0 203.5 jit_solution(13947096180868856419)
XLA Ops:
  10.7 2.2 %fusion.65 = (f32[8,1,1,3072]{3,2,1,0:T(1,128)}, f32[8,1,1,3072]{3,2,1,0:T(1,128)S(1)}, f32[8,1,1,3072]{3,2,1,0:T(1,128)}, f32[8,1,1,3072]{3,2,1,0:T(1,128)}) fusion(f32[8,2,2,3072]{3,2,1,0:T(2,128)} %param.16), kind=kLoop, calls=%fused_computation.172 | loop fusion | bytes 786432 | tf_op jit(solution)/shard_map/slice | solution.py:118
  14.4 2.0 fusion.16
  24.3 5.2 %all-to-all-start = ((bf16[4,2,8,3072]{3,2,1,0:T(8,128)(2,1)}), bf16[4,2,8,3072]{3,2,1,0:T(8,128)(2,1)}, u32[]{:S(2)}, u32[]{:S(2)}) async-start(bf16[4,2,8,3072]{3,2,1,0:T(8,128)(2,1)} %copy.121), calls=%async_computation | async-start | bytes 786432 | tf_op jit(solution)/shard_map/all_to_all | solution.py:142
  30.0 1.5 fusion.13
  31.5 2.2 %fusion.14 = bf16[64,3072]{1,0:T(8,128)(2,1)} fusion(f32[64,3072]{1,0:T(8,128)S(1)} %fusion.13, f32[8,1,1,3072]{3,2,1,0:T(1,128)} %get-tuple-element.151, s32[64]{0:T(128)S(1)} %dynamic_slice.28), kind=kOutput, calls=%fused_computation.30 | convolution fusion | flops 19268096 | bytes 1278208 | tf_op jit(solution)/shard_map/dot_general | solution.py:57
  38.3 4.5 %gather_fusion.3 = bf16[4,2,64,768]{3,2,1,0:T(8,128)(2,1)} fusion(bf16[32,2,64,768]{3,2,1,0:T(8,128)(2,1)} %param.20, s32[1024]{0:T(1024)} %copy-done.14), kind=kCustom, calls=%fused_computation.3 | custom fusion | bytes 1572880 | tf_op jit(solution)/shard_map/jit(_take)/gather | solution.py:138
  42.8 2.2 %select_select_fusion = bf16[4,2,64,768]{3,2,1,0:T(8,128)(2,1)} fusion(bf16[4,2,64,768]{3,2,1,0:T(8,128)(2,1)} %gather_fusion.3, pred[4]{0:T(512)(128)(4,1)S(1)} %copy-done.20, pred[4]{0:T(512)(128)(4,1)} %copy-done.16), kind=kLoop, calls=%fused_computation.50 | loop fusion | flops 786432 | bytes 1572872 | tf_op jit(solution)/shard_map/jit(_where)/select_n | solution.py:136
  45.0 4.2 %all-to-all-start.1 = ((bf16[4,2,64,768]{3,2,1,0:T(8,128)(2,1)}), bf16[4,2,64,768]{3,2,1,0:T(8,128)(2,1)}, u32[]{:S(2)}, u32[]{:S(2)}) async-start(bf16[4,2,64,768]{3,2,1,0:T(8,128)(2,1)} %select_select_fusion), calls=%async_computation.1 | async-start | bytes 1572864 | tf_op jit(solution)/shard_map/all_to_all | solution.py:143
  49.2 2.3 %gather_fusion.2 = bf16[4,2,8,3072]{3,2,1,0:T(8,128)(2,1)} fusion(bf16[4,2,8,3072]{3,2,1,0:T(8,128)(2,1)} %all-to-all-done, s32[1024]{0:T(1024)S(1)} %pad_clamp_fusion), kind=kCustom, calls=%fused_computation.2 | custom fusion | bytes 786448 | tf_op jit(solution)/shard_map/jit(_take)/gather | solution.py:146
  52.6 7.9 %all-to-all-done.1 = bf16[4,2,64,768]{3,2,1,0:T(8,128)(2,1)} async-done(((bf16[4,2,64,768]{3,2,1,0:T(8,128)(2,1)}), bf16[4,2,64,768]{3,2,1,0:T(8,128)(2,1)}, u32[]{:S(2)}, u32[]{:S(2)}) %all-to-all-start.1) | async-done | bytes 786464 | tf_op jit(solution)/shard_map/all_to_all | solution.py:143
  60.6 2.8 %gather_fusion.4 = bf16[4,2,64,768]{3,2,1,0:T(8,128)(2,1)} fusion(bf16[4,2,64,768]{3,2,1,0:T(8,128)(2,1)} %all-to-all-done.1, s32[1024]{0:T(1024)} %copy-done.15), kind=kCustom, calls=%fused_computation.4 | custom fusion | bytes 1572880 | tf_op jit(solution)/shard_map/jit(_take)/gather | solution.py:147
  65.6 2.0 fusion.30
  67.6 14.9 %all_gather.15 = bf16[64,256]{1,0:T(8,128)(2,1)S(1)} all-gather(bf16[8,256]{1,0:T(8,128)(2,1)S(1)} %fusion.30), channel_id=1, replica_groups=mesh['bag'=4,'seq'=8] {'seq'}, dimensions={0}, use_global_device_ids=true | all-gather | bytes 36864 | tf_op jit(solution)/shard_map/all_gather | solution.py:156
  83.2 4.2 %fusion.7 = f32[256,768]{1,0:T(8,128)S(1)} fusion(bf16[256,3072]{1,0:T(8,128)(2,1)} %all-gather.5.cloned.1.call-done, bf16[2,3072,768]{2,1,0:T(8,128)(2,1)} %param.17), kind=kOutput, calls=%fused_computation.21 | convolution fusion | flops 1207959552 | bytes 7077888 | tf_op jit(solution)/shard_map/dot_general | solution.py:69
  88.6 2.3 %copy.126 = f32[256,768]{0,1:T(8,128)} copy(f32[256,768]{1,0:T(8,128)} %convolution_add_fusion.5) | data formatting | bytes 1572864 | tf_op jit(solution)/shard_map/add | solution.py:76
  92.1 1.6 fusion.41
  93.7 1.5 multiply_convert_fusion.2
  95.2 3.1 %fusion.24 = bf16[8,512]{1,0:T(8,128)(2,1)S(1)} fusion(bf16[512,3072]{1,0:T(8,128)(2,1)} %all-gather.3.cloned.1.call-done, bf16[4,2,8,3072]{3,2,0,1:T(8,128)(2,1)S(1)} %copy_select_fusion, f32[4,512]{1,0:T(4,128)S(1)} %fusion.47), kind=kOutput, calls=%fused_computation.42 | convolution fusion | flops 100691968 | bytes 3358720 | tf_op jit(solution)/shard_map/nd,urd->urn/dot_general | solution.py:61
  98.3 14.2 %all_gather.13 = bf16[64,512]{1,0:T(8,128)(2,1)S(1)} all-gather(bf16[8,512]{1,0:T(8,128)(2,1)S(1)} %fusion.24), channel_id=1, replica_groups=mesh['bag'=4,'seq'=8] {'seq'}, dimensions={0}, use_global_device_ids=true | all-gather | bytes 73728 | tf_op jit(solution)/shard_map/all_gather | solution.py:155
  112.5 5.0 %fusion.9 = f32[512,768]{1,0:T(8,128)S(1)} fusion(bf16[512,3072]{1,0:T(8,128)(2,1)S(1)} %copy-done.3, bf16[2,3072,768]{2,1,0:T(8,128)(2,1)} %param.17), kind=kOutput, calls=%fused_computation.23 | convolution fusion | flops 2415919104 | bytes 9437184 | tf_op jit(solution)/shard_map/dot_general | solution.py:69
  117.5 1.6 convolution_add_fusion.4
  119.1 3.1 %copy.123 = f32[512,768]{0,1:T(8,128)} copy(f32[512,768]{1,0:T(8,128)} %convolution_add_fusion.4) | data formatting | bytes 3145728 | tf_op jit(solution)/shard_map/add | solution.py:76
  128.4 26.8 %while.23 = (s32[]{:T(128)}, bf16[2,768,128]{2,1,0:T(8,128)(2,1)}, bf16[2,768,128]{1,2,0:T(8,128)(2,1)}, s32[768]{0:T(1024)S(1)}, bf16[2,768,128]{1,2,0:T(8,128)...) while((s32[]{:T(128)}, bf16[2,768,128]{2,1,0:T(8,128)(2,1)}, ...), condition=%wide.wide.region_19.20_spmd, body=%wide.wide.region_14.19_spmd.sunk | while | flops 102465024 | bytes 5647666 | solution.py:175
  132.2 8.0 %while.24 = (s32[]{:T(128)}, bf16[3,256,128]{2,1,0:T(8,128)(2,1)}, s32[3,256]{1,0:T(4,128)S(1)}, s32[768]{0:T(1024)S(1)}, bf16[3,256,128]{2,1,0:T(8,128)(2,1)}, ...) while((s32[]{:T(128)}, bf16[3,256,128]{2,1,0:T(8,128)(2,1)}, ...), condition=%wide.region_18.18_spmd, body=%wide.region_15.17_spmd.sunk | while | flops 102465024 | bytes 2894953 | solution.py:49
  140.1 1.6 bitcast_dynamic-update-slice_fusion.3
  145.6 8.0 %while.24 = (s32[]{:T(128)}, bf16[3,256,128]{2,1,0:T(8,128)(2,1)}, s32[3,256]{1,0:T(4,128)S(1)}, s32[768]{0:T(1024)S(1)}, bf16[3,256,128]{2,1,0:T(8,128)(2,1)}, ...) while((s32[]{:T(128)}, bf16[3,256,128]{2,1,0:T(8,128)(2,1)}, ...), condition=%wide.region_18.18_spmd, body=%wide.region_15.17_spmd.sunk | while | flops 102465024 | bytes 2894953 | solution.py:49
  153.6 1.6 bitcast_dynamic-update-slice_fusion.3
  156.1 1.5 fusion.64
  158.5 4.7 %all-to-all-start.3 = ((bf16[8,32,256]{2,1,0:T(8,128)(2,1)}), bf16[8,32,256]{2,1,0:T(8,128)(2,1)S(1)}, u32[]{:S(2)}, u32[]{:S(2)}) async-start(bf16[8,32,256]{2,1,0:T(8,128)(2,1)} %all_to_all.26), calls=%async_computation.3 | async-start | bytes 262144 | tf_op jit(solution)/shard_map/all_to_all | solution.py:180
  176.1 1.4 copy.139
  181.1 5.1 %all-to-all-start.2 = ((bf16[8,64,256]{2,1,0:T(8,128)(2,1)}), bf16[8,64,256]{2,1,0:T(8,128)(2,1)S(1)}, u32[]{:S(2)}, u32[]{:S(2)}) async-start(bf16[8,64,256]{2,1,0:T(8,128)(2,1)} %copy-done.9), calls=%async_computation.2 | async-start | bytes 524288 | tf_op jit(solution)/shard_map/all_to_all | solution.py:14
  186.9 9.0 %all-to-all-done.2 = bf16[8,64,256]{2,1,0:T(8,128)(2,1)S(1)} async-done(((bf16[8,64,256]{2,1,0:T(8,128)(2,1)}), bf16[8,64,256]{2,1,0:T(8,128)(2,1)S(1)}, u32[]{:S(2)}, u32[]{:S(2)}) %all-to-all-start.2) | async-done | bytes 262176 | tf_op jit(solution)/shard_map/all_to_all | solution.py:14
  (180 shorter events, 73.7 us)
Async XLA Ops:
  7.2 13.2 %copy-start = (bf16[32,2,8,3072]{3,2,1,0:T(8,128)(2,1)S(1)}, bf16[32,2,8,3072]{3,2,1,0:T(8,128)(2,1)}, u32[]{:S(2)}) copy-start(bf16[32,2,8,3072]{3,2,1,0:T(8,128)(2,1)} %param.19) | copy-start | bytes 9437188
  7.2 11.8 %copy-start.10 = (s32[4,4]{1,0:T(4,128)S(1)}, s32[4,4]{1,0:T(4,128)}, u32[]{:S(2)}) copy-start(s32[4,4]{1,0:T(4,128)} %param.22) | copy-start | bytes 196
  7.2 11.1 %copy-start.1 = (s32[128]{0:T(128)S(1)}, s32[128]{0:T(128)}, u32[]{:S(2)}) copy-start(s32[128]{0:T(128)} %param.21) | copy-start | bytes 1540
  7.2 58.4 %all-gather.5.cloned.1.call-start = ((), (), s32[]{:S(2)}) async-start(), calls=%async_computation.5 | async-start | bytes 1769472 | tf_op jit(solution)/shard_map/all_gather | solution.py:150
  10.7 2.3 %copy-start.17 = (s32[256]{0:T(256)}, s32[256]{0:T(256)S(1)}, u32[]{:S(2)}) copy-start(s32[256]{0:T(256)S(1)} %convert_reduce_fusion.2) | copy-start | bytes 3076
  14.4 15.2 %copy-start.2 = (bf16[64,3072]{1,0:T(8,128)(2,1)S(1)}, bf16[64,3072]{1,0:T(8,128)(2,1)}, u32[]{:S(2)}) copy-start(bf16[64,3072]{1,0:T(8,128)(2,1)} %param.14) | copy-start | bytes 1179652
  19.7 13.9 %copy-start.16 = (pred[4]{0:T(512)(128)(4,1)}, pred[4]{0:T(512)(128)(4,1)S(1)}, u32[]{:S(2)}) copy-start(pred[4]{0:T(512)(128)(4,1)S(1)} %get-tuple-element.130) | copy-start | bytes 16
  19.9 0.5 copy-start.23
  20.4 13.3 %copy-start.14 = (s32[1024]{0:T(1024)}, s32[1024]{0:T(1024)S(1)}, u32[]{:S(2)}) copy-start(s32[1024]{0:T(1024)S(1)} %pad_clamp_fusion.1) | copy-start | bytes 12292
  21.7 12.0 %copy-start.18 = (s32[256]{0:T(256)S(1)}, s32[256]{0:T(256)}, u32[]{:S(2)}) copy-start(s32[256]{0:T(256)} %copy-done.17) | copy-start | bytes 3076
  22.4 7.1 %copy-start.19 = (pred[4]{0:T(512)(128)(4,1)}, pred[4]{0:T(512)(128)(4,1)S(1)}, u32[]{:S(2)}) copy-start(pred[4]{0:T(512)(128)(4,1)S(1)} %compare_and_fusion) | copy-start | bytes 16
  24.3 20.7 %all-to-all-start = ((bf16[4,2,8,3072]{3,2,1,0:T(8,128)(2,1)}), bf16[4,2,8,3072]{3,2,1,0:T(8,128)(2,1)}, u32[]{:S(2)}, u32[]{:S(2)}) async-start(bf16[4,2,8,3072]{3,2,1,0:T(8,128)(2,1)} %copy.121), calls=%async_computation | async-start | bytes 786432 | tf_op jit(solution)/shard_map/all_to_all | solution.py:142
  29.5 65.7 %all-gather.3.cloned.1.call-start = ((), (), s32[]{:S(2)}) async-start(), calls=%async_computation.4 | async-start | bytes 3538944 | tf_op jit(solution)/shard_map/all_gather | solution.py:149
  31.5 11.3 %copy-start.20 = (pred[4]{0:T(512)(128)(4,1)S(1)}, pred[4]{0:T(512)(128)(4,1)}, u32[]{:S(2)}) copy-start(pred[4]{0:T(512)(128)(4,1)} %copy-done.19) | copy-start | bytes 16
  33.8 15.4 %copy-start.11 = (s32[768]{0:T(1024)}, s32[768]{0:T(1024)S(1)}, u32[]{:S(2)}) copy-start(s32[768]{0:T(1024)S(1)} %pad_add_fusion) | copy-start | bytes 9220
  34.5 14.8 %copy-start.15 = (s32[1024]{0:T(1024)}, s32[1024]{0:T(1024)S(1)}, u32[]{:S(2)}) copy-start(s32[1024]{0:T(1024)S(1)} %pad_clamp_fusion) | copy-start | bytes 12292
  45.0 15.6 %all-to-all-start.1 = ((bf16[4,2,64,768]{3,2,1,0:T(8,128)(2,1)}), bf16[4,2,64,768]{3,2,1,0:T(8,128)(2,1)}, u32[]{:S(2)}, u32[]{:S(2)}) async-start(bf16[4,2,64,768]{3,2,1,0:T(8,128)(2,1)} %select_select_fusion), calls=%async_computation.1 | async-start | bytes 1572864 | tf_op jit(solution)/shard_map/all_to_all | solution.py:143
  83.2 4.3 %copy-start.5 = (bf16[4,1,64,768]{3,2,1,0:T(8,128)(2,1)S(1)}, bf16[4,1,64,768]{3,2,1,0:T(8,128)(2,1)}, u32[]{:S(2)}) copy-start(bf16[4,1,64,768]{3,2,1,0:T(8,128)(2,1)} %get-tuple-element.142) | copy-start | bytes 1179652
  90.9 21.5 %copy-start.13 = (bf16[512,4]{0,1:T(4,128)(2,1)S(1)}, bf16[512,4]{0,1:T(4,128)(2,1)}, u32[]{:S(2)}) copy-start(bf16[512,4]{0,1:T(4,128)(2,1)} %fusion.46) | copy-start | bytes 12292
  95.2 17.3 %copy-start.3 = (bf16[512,3072]{1,0:T(8,128)(2,1)S(1)}, bf16[512,3072]{1,0:T(8,128)(2,1)}, u32[]{:S(2)}) copy-start(bf16[512,3072]{1,0:T(8,128)(2,1)} %all-gather.3.cloned.1.call-done) | copy-start | bytes 9437188
  112.5 5.0 %copy-start.4 = (bf16[4,1,64,768]{3,2,1,0:T(8,128)(2,1)S(1)}, bf16[4,1,64,768]{3,2,1,0:T(8,128)(2,1)}, u32[]{:S(2)}) copy-start(bf16[4,1,64,768]{3,2,1,0:T(8,128)(2,1)} %get-tuple-element.141) | copy-start | bytes 1179652
  119.1 5.6 %copy-start.21 = (f32[128]{0:T(128)S(1)}, f32[128]{0:T(128)}, u32[]{:S(2)}) copy-start(f32[128]{0:T(128)} %get-tuple-element.155) | copy-start | bytes 1540
  119.1 5.6 %copy-start.22 = (f32[128]{0:T(128)S(1)}, f32[128]{0:T(128)}, u32[]{:S(2)}) copy-start(f32[128]{0:T(128)} %get-tuple-element.157) | copy-start | bytes 1540
  119.1 6.9 %copy-start.8 = (bf16[256,2,128]{0,2,1:T(8,128)(2,1)S(1)}, bf16[256,2,128]{0,2,1:T(8,128)(2,1)}, u32[]{:S(2)}) copy-start(bf16[256,2,128]{0,2,1:T(8,128)(2,1)} %get-tuple-element.159) | copy-start | bytes 393220
  119.1 7.7 %copy-start.6 = (bf16[256,2,128]{0,2,1:T(8,128)(2,1)S(1)}, bf16[256,2,128]{0,2,1:T(8,128)(2,1)}, u32[]{:S(2)}) copy-start(bf16[256,2,128]{0,2,1:T(8,128)(2,1)} %fusion.41) | copy-start | bytes 393220
  122.2 5.4 %copy-start.7 = (bf16[256,2,128]{0,2,1:T(8,128)(2,1)S(1)}, bf16[256,2,128]{0,2,1:T(8,128)(2,1)}, u32[]{:S(2)}) copy-start(bf16[256,2,128]{0,2,1:T(8,128)(2,1)} %get-tuple-element.160) | copy-start | bytes 393220
  122.2 6.2 %copy-start.12 = (s32[768]{0:T(1024)S(1)}, s32[768]{0:T(1024)}, u32[]{:S(2)}) copy-start(s32[768]{0:T(1024)} %copy-done.11) | copy-start | bytes 9220
  158.5 22.6 %all-to-all-start.3 = ((bf16[8,32,256]{2,1,0:T(8,128)(2,1)}), bf16[8,32,256]{2,1,0:T(8,128)(2,1)S(1)}, u32[]{:S(2)}, u32[]{:S(2)}) async-start(bf16[8,32,256]{2,1,0:T(8,128)(2,1)} %all_to_all.26), calls=%async_computation.3 | async-start | bytes 262144 | tf_op jit(solution)/shard_map/all_to_all | solution.py:180
  180.4 0.7 copy-start.9
  181.1 14.8 %all-to-all-start.2 = ((bf16[8,64,256]{2,1,0:T(8,128)(2,1)}), bf16[8,64,256]{2,1,0:T(8,128)(2,1)S(1)}, u32[]{:S(2)}, u32[]{:S(2)}) async-start(bf16[8,64,256]{2,1,0:T(8,128)(2,1)} %copy-done.9), calls=%async_computation.2 | async-start | bytes 524288 | tf_op jit(solution)/shard_map/all_to_all | solution.py:14
Sparse Core Ops, SparseCore 0:
  16.5 27.9 all-gather.4
  46.2 37.6 all-gather.2
